TPU v7x, 256 devices: a whole 4x4x8 slice. The times are simulated.
256 devices in a mesh: rep: 2 (over z_hi), dp: 32 (over z_lo, x, core), mp: 4 (over y).
Axes of the slice: x: 4, y: 4, z: 8 (z_hi: 2, z_lo: 4; z = z_hi * 4 + z_lo), core: 2. Of those that a mesh axis runs over, the one named last changes fastest.
Arguments:
- tokens: bfloat16 [24576, 2048], P(('rep', 'dp', 'mp')), may hold values from -6 to 6
- request_ids: int32 [64, 384], P(('rep', 'dp')), may hold values from 0 to 7, never falling along the last dimension, each value on 1 to 192 neighbouring positions
- cache_entries: bfloat16 [32768, 4096], P(('rep', 'dp', 'mp')), may hold values from -250 to 250, as said below
- cached_lengths: int32 [64, 8], replicated, may hold values from 1 to 256, 512 in all within a row
- traded: int32 [32], P('dp'), may hold values from 0 to 1, as said below
- query_weight: bfloat16 [2048, 2048], P(None, 'mp'), may hold values from -0.125 to 0.125
- key_weight: bfloat16 [2048, 2048], P(None, 'mp'), may hold values from -0.125 to 0.125
- value_weight: bfloat16 [2048, 2048], P(None, 'mp'), may hold values from -0.125 to 0.125
- output_weight: bfloat16 [2048, 2048], P('mp'), may hold values from -0.125 to 0.125
- gate_weight: bfloat16 [2048, 8192], P('dp', 'mp'), may hold values from -0.125 to 0.125
- up_weight: bfloat16 [2048, 8192], P('dp', 'mp'), may hold values from -0.125 to 0.125
- down_weight: bfloat16 [2048, 8192], P('dp', 'mp'), may hold values from -0.0625 to 0.0625
Outputs:
- layer_output: bfloat16 [24576, 2048], P(('rep', 'dp', 'mp'))
Inputs may be any that keep to these rules, and one draw needn't show every extreme that they name: `request_ids`: each group's row never falls; every request 0 to 7 has 1 to 192 new tokens in each group, some request exactly 192. `cached_lengths`: each row sums to 512; its largest entry is 256. `traded`: exactly 16 entries are 1. `cache_entries`: keys are stored already rotated to their positions; rows of cache group g are g * 512 to (g + 1) * 512 - 1, the requests' prefixes in request order.
All inputs are finite; a program needn't handle non-finite values.
Results may differ from a plain program's by a relative error of at most 0.013.
The roundings to bfloat16 on the way count: a program that leaves them out, or rounds other values in their place, can miss the bound.
Values may be sent and summed in bfloat16 or wider, within the bound.
A program may use at most 128 MiB of HBM per device.

v0:
```python
import math
import jax
import jax.numpy as jnp
from jax import lax
from jax.sharding import PartitionSpec as P

D = 2048
HEADS = 16
HEAD_DIM = 128
TOK_GROUP = 384
CACHE = 512
EPSILON = 1e-05
ROPE_BASE = 10000.0


def swapped(value, axis, apart):
    mask = 2**apart
    pairs = [(source, source ^ mask) for source in range(lax.axis_size(axis))]
    return lax.ppermute(value, axis, pairs)


def layer_norm(rows):
    center = rows - jnp.mean(rows, axis=-1, keepdims=True)
    spread = jnp.mean(center * center, axis=-1, keepdims=True)
    return center * lax.rsqrt(spread + EPSILON)


def request_layout(request_row, length_row, cache_size):
    number = length_row.shape[0]
    labels = jnp.arange(number, dtype=jnp.int32)
    onehot = (request_row[:, None] == labels[None, :]).astype(jnp.int32)
    counts = jnp.sum(onehot, axis=0)
    starts = jnp.cumsum(counts) - counts
    token_place = jnp.arange(request_row.shape[0], dtype=jnp.int32)
    positions = jnp.sum(onehot * (length_row - starts)[None, :], axis=1) + token_place
    bounds = jnp.cumsum(length_row)
    cache_place = jnp.arange(cache_size, dtype=jnp.int32)
    owner = jnp.sum((cache_place[:, None] >= bounds[None, :]).astype(jnp.int32), axis=1)
    return (positions, owner)


def rotate(vectors, positions):
    half = vectors.shape[-1] // 2
    freq = ROPE_BASE ** (-jnp.arange(half, dtype=jnp.float32) / half)
    angle = positions.astype(jnp.float32)[:, None] * freq[None, :]
    cosine = jnp.cos(angle)[:, None, :]
    sine = jnp.sin(angle)[:, None, :]
    first = vectors[..., :half]
    second = vectors[..., half:]
    return jnp.concatenate(
        [first * cosine - second * sine, second * cosine + first * sine], axis=-1
    )


def attend(query, keys_new, values_new, keys_cache, values_cache, request_row, owner):
    scale = 1.0 / math.sqrt(query.shape[-1])
    keys = jnp.concatenate([keys_cache, keys_new], axis=0)
    values = jnp.concatenate([values_cache, values_new], axis=0)
    scores = jnp.einsum("thd,khd->htk", query, keys, preferred_element_type=jnp.float32) * scale
    count = request_row.shape[0]
    place = jnp.arange(count, dtype=jnp.int32)
    same_cache = owner[None, :] == request_row[:, None]
    same_new = (request_row[None, :] == request_row[:, None]) & (place[None, :] <= place[:, None])
    allowed = jnp.concatenate([same_cache, same_new], axis=1)
    scores = jnp.where(allowed[None], scores, -1e30)
    top = jnp.max(scores, axis=-1, keepdims=True)
    raised = jnp.exp(scores - top)
    total = jnp.sum(raised, axis=-1, keepdims=True)
    weights = (raised / total).astype(jnp.bfloat16)
    mixed = jnp.einsum("htk,khd->thd", weights, values, preferred_element_type=jnp.float32)
    return mixed.astype(jnp.bfloat16)


def local(
    tokens,
    request_ids,
    cache_entries,
    cached_lengths,
    traded,
    query_weight,
    key_weight,
    value_weight,
    output_weight,
    gate_weight,
    up_weight,
    down_weight,
):
    tensor_size = lax.axis_size("mp")
    local_heads = HEADS // tensor_size
    replica = lax.axis_index("rep")
    within = lax.axis_index("dp")
    pairs = lax.axis_size("dp")
    group = replica * pairs + within
    moved_here = traded[0] == 1
    source = jnp.where(moved_here, (1 - replica) * pairs + within, group)
    length_row = lax.dynamic_slice_in_dim(cached_lengths, source, 1, 0)[0]
    request_row = request_ids[0]
    partner = swapped(cache_entries, "rep", 0)
    stored = jnp.where(moved_here, partner, cache_entries)
    by_heads = lax.all_to_all(
        stored.reshape(stored.shape[0], 2, D), "mp", split_axis=2, concat_axis=0, tiled=True
    )
    keys_cache = by_heads[:, 0].reshape(CACHE, local_heads, HEAD_DIM)
    values_cache = by_heads[:, 1].reshape(CACHE, local_heads, HEAD_DIM)
    rows_full = lax.all_gather(tokens, "mp", axis=0, tiled=True)
    positions, owner = request_layout(request_row, length_row, CACHE)
    normed = layer_norm(rows_full.astype(jnp.float32)).astype(jnp.bfloat16)
    query = jnp.dot(normed, query_weight, preferred_element_type=jnp.float32).reshape(
        TOK_GROUP, local_heads, HEAD_DIM
    )
    query = rotate(query, positions).astype(jnp.bfloat16)
    keys_new = jnp.dot(normed, key_weight, preferred_element_type=jnp.float32).reshape(
        TOK_GROUP, local_heads, HEAD_DIM
    )
    keys_new = rotate(keys_new, positions).astype(jnp.bfloat16)
    values_new = (
        jnp.dot(normed, value_weight, preferred_element_type=jnp.float32)
        .astype(jnp.bfloat16)
        .reshape(TOK_GROUP, local_heads, HEAD_DIM)
    )
    mixed = attend(query, keys_new, values_new, keys_cache, values_cache, request_row, owner)
    mixed = mixed.reshape(TOK_GROUP, local_heads * HEAD_DIM)
    own_sum = lax.psum_scatter(
        jnp.dot(mixed, output_weight, preferred_element_type=jnp.float32),
        "mp",
        scatter_dimension=0,
        tiled=True,
    )
    state_own = (tokens.astype(jnp.float32) + own_sum).astype(jnp.bfloat16)
    normed_own = layer_norm(state_own.astype(jnp.float32)).astype(jnp.bfloat16)
    normed_two = lax.all_gather(normed_own, "mp", axis=0, tiled=True)

    def add_rows(piece):
        return jnp.dot(normed_two, piece, preferred_element_type=jnp.float32)

    gate = add_rows(lax.all_gather(gate_weight, "dp", axis=0, tiled=True))
    upward = add_rows(lax.all_gather(up_weight, "dp", axis=0, tiled=True))
    activated = (jax.nn.silu(gate) * upward).astype(jnp.bfloat16)
    terms = lax.dot_general(
        activated,
        lax.all_gather(down_weight, "dp", axis=0, tiled=True),
        (((1,), (1,)), ((), ())),
        preferred_element_type=jnp.float32,
    )
    hidden_own = lax.psum_scatter(terms, "mp", scatter_dimension=0, tiled=True)
    return (state_own.astype(jnp.float32) + hidden_own).astype(jnp.bfloat16)


def solution(mesh):
    in_specs = (
        P(("rep", "dp", "mp"), None),
        P(("rep", "dp"), None),
        P(("rep", "dp", "mp"), None),
        P(),
        P("dp"),
        P(None, "mp"),
        P(None, "mp"),
        P(None, "mp"),
        P("mp", None),
        P("dp", "mp"),
        P("dp", "mp"),
        P("dp", "mp"),
    )
    out_specs = P(("rep", "dp", "mp"), None)
    return jax.shard_map(local, mesh=mesh, in_specs=in_specs, out_specs=out_specs, check_vma=False)
```

profile of v0, /device:TPU:1, one launch (start us, length us, event | category | flops | bytes accessed | tf_op | source)
XLA Modules:
  0.0 476.3 jit_solution(9177185737929228484)
XLA Ops:
  8.3 7.8 %collective-permute-start = (bf16[128,4096]{0,1:T(8,128)(2,1)S(1)}, bf16[128,4096]{0,1:T(8,128)(2,1)}, u32[]{:S(2)}, u32[]{:S(2)}) collective-permute-start(bf16[128,4096]{0,1:T(8,128)(2,1)S(1)} %copy.71), channel_id=1, source_target_pairs={{0,128},{128,0},{1,129},{129,1},{2,130},{130,2},{3,131},{131,3},{4... | collective-permute-start | bytes 3145736 | tf_op jit(solution)/shard_map/ppermute | solution.py:19
  19.2 25.3 %collective-permute-done = bf16[128,4096]{0,1:T(8,128)(2,1)} collective-permute-done((bf16[128,4096]{0,1:T(8,128)(2,1)S(1)}, bf16[128,4096]{0,1:T(8,128)(2,1)}, u32[]{:S(2)}, u32[]{:S(2)}) %collective-permute-start) | collective-permute-done | bytes 1048608 | tf_op jit(solution)/shard_map/ppermute | solution.py:19
  45.9 9.5 %copy.73 = bf16[128,2,2048]{0,1,2:T(2,128)(2,1)} copy(bf16[128,2,2048]{0,2,1:T(8,128)(2,1)S(1)} %bitcast.28) | data formatting | bytes 2097152 | tf_op jit(solution)/shard_map/reshape | solution.py:101
  55.4 4.7 all-to-all-start
  62.5 7.3 %all-to-all-done = bf16[128,2,2048]{0,1,2:T(2,128)(2,1)S(1)} async-done(((bf16[128,2,2048]{0,1,2:T(2,128)(2,1)}), bf16[128,2,2048]{0,1,2:T(2,128)(2,1)S(1)}, u32[]{:S(2)}, u32[]{:S(2)}) %all-to-all-start) | async-done | bytes 1048608 | tf_op jit(solution)/shard_map/all_to_all | solution.py:100
  75.0 2.0 copy.76
  78.9 2.0 fusion.4
  80.8 3.6 fusion.35
  85.8 4.0 fusion.37
  89.8 2.3 reshape.151
  92.1 3.9 convolution_convert_fusion
  95.9 1.9 copy.85
  97.8 2.3 fusion.41
  101.6 2.7 fusion.43
  105.4 2.7 fusion.44
  108.4 61.6 %reduce-scatter.3.cloned.1.call-done = f32[96,2048]{1,0:T(8,128)} async-done(((f32[384,2048]{1,0:T(8,128)}), f32[96,2048]{1,0:T(8,128)}) %reduce-scatter.3.cloned.1.call-update) | async-done | bytes 786448 | tf_op jit(solution)/shard_map/reduce_scatter | solution.py:123
  174.4 27.1 %all-gather.8.cloned.1.call-done = bf16[384,2048]{1,0:T(8,128)(2,1)} async-done(((bf16[96,2048]{1,0:T(8,128)(2,1)}), bf16[384,2048]{1,0:T(8,128)(2,1)}) %all-gather.8.cloned.1.call-update) | async-done | bytes 1572880 | tf_op jit(solution)/shard_map/all_gather | solution.py:131
  201.5 71.4 %all-gather.10.cloned.1.call-done = bf16[2048,2048]{1,0:T(8,128)(2,1)} async-done(((bf16[64,2048]{1,0:T(8,128)(2,1)}), bf16[2048,2048]{1,0:T(8,128)(2,1)}) %all-gather.10.cloned.1.call-update) | async-done | bytes 8388624 | tf_op jit(solution)/shard_map/all_gather | solution.py:136
  272.9 9.0 %fusion.45 = f32[384,2048]{1,0:T(8,128)} fusion(bf16[384,2048]{1,0:T(8,128)(2,1)} %all-gather.8.cloned.1.call-done, bf16[2048,2048]{1,0:T(8,128)(2,1)} %all-gather.10.cloned.1.call-done), kind=kOutput, calls=%fused_computation.76 | convolution fusion | flops 3221225472 | bytes 13107200 | tf_op jit(solution)/shard_map/dot_general | solution.py:134
  281.9 60.6 %all-gather.12.cloned.1.call-done = bf16[2048,2048]{1,0:T(8,128)(2,1)} async-done(((bf16[64,2048]{1,0:T(8,128)(2,1)}), bf16[2048,2048]{1,0:T(8,128)(2,1)}) %all-gather.12.cloned.1.call-update) | async-done | bytes 8388624 | tf_op jit(solution)/shard_map/all_gather | solution.py:137
  342.5 69.7 %all-gather.14.cloned.1.call-done = bf16[2048,2048]{1,0:T(8,128)(2,1)} async-done(((bf16[64,2048]{1,0:T(8,128)(2,1)}), bf16[2048,2048]{1,0:T(8,128)(2,1)}) %all-gather.14.cloned.1.call-update) | async-done | bytes 8388624 | tf_op jit(solution)/shard_map/all_gather | solution.py:141
  412.2 15.9 %fusion.25 = f32[384,2048]{1,0:T(8,128)} fusion(bf16[2048,2048]{1,0:T(8,128)(2,1)} %all-gather.14.cloned.1.call-done, f32[384,2048]{1,0:T(8,128)} %fusion.45, bf16[384,2048]{1,0:T(8,128)(2,1)} %all-gather.8.cloned.1.call-done, bf16[2048,2048]{1,0:T(8,128)(2,1)} %all-gather.12.cloned.1.call-done), kind=kOutput, calls=%fused_computation.42 | convolution fusion | flops 6447169536 | bytes 24641536 | tf_op jit(solution)/shard_map/dot_general | solution.py:139
  428.1 39.4 %reduce-scatter.5.cloned.1.call-done = f32[96,2048]{1,0:T(8,128)} async-done(((f32[384,2048]{1,0:T(8,128)}), f32[96,2048]{1,0:T(8,128)}) %reduce-scatter.5.cloned.1.call-update) | async-done | bytes 786448 | tf_op jit(solution)/shard_map/reduce_scatter | solution.py:145
  467.5 2.0 fusion.24
  (67 shorter events, 23.4 us)
Async XLA Ops:
  6.5 98.8 %copy-start = (bf16[512,2048]{1,0:T(8,128)(2,1)S(1)}, bf16[512,2048]{1,0:T(8,128)(2,1)}, u32[]{:S(2)}) copy-start(bf16[512,2048]{1,0:T(8,128)(2,1)} %param.20) | copy-start | bytes 6291460
  6.5 70.5 %all-gather.6.cloned.1.call-start = ((), (), s32[]{:S(2)}) async-start(), calls=%async_computation.3 | async-start | bytes 1966080 | tf_op jit(solution)/shard_map/all_gather | solution.py:105
  8.3 36.3 %collective-permute-start = (bf16[128,4096]{0,1:T(8,128)(2,1)S(1)}, bf16[128,4096]{0,1:T(8,128)(2,1)}, u32[]{:S(2)}, u32[]{:S(2)}) collective-permute-start(bf16[128,4096]{0,1:T(8,128)(2,1)S(1)} %copy.71), channel_id=1, source_target_pairs={{0,128},{128,0},{1,129},{129,1},{2,130},{130,2},{3,131},{131,3},{4... | collective-permute-start | bytes 3145736 | tf_op jit(solution)/shard_map/ppermute | solution.py:19
  55.4 14.5 %all-to-all-start = ((bf16[128,2,2048]{0,1,2:T(2,128)(2,1)}), bf16[128,2,2048]{0,1,2:T(2,128)(2,1)S(1)}, u32[]{:S(2)}, u32[]{:S(2)}) async-start(bf16[128,2,2048]{0,1,2:T(2,128)(2,1)} %copy.73), calls=%async_computation | async-start | bytes 2097152 | tf_op jit(solution)/shard_map/all_to_all | solution.py:100
  60.1 109.8 %reduce-scatter.3.cloned.1.call-start = ((), (), s32[]{:S(2)}) async-start(), calls=%async_computation.4 | async-start | bytes 3932160 | tf_op jit(solution)/shard_map/reduce_scatter | solution.py:123
  77.0 3.8 copy-start.2
  97.8 2.3 copy-start.4
  97.8 2.3 copy-start.5
  100.6 1.0 copy-start.8
  101.6 2.7 copy-start.6
  101.6 2.7 copy-start.7
  105.4 64.5 %copy-start.3 = (bf16[96,2048]{1,0:T(8,128)(2,1)S(1)}, bf16[96,2048]{1,0:T(8,128)(2,1)}, u32[]{:S(2)}) copy-start(bf16[96,2048]{1,0:T(8,128)(2,1)} %param.12) | copy-start | bytes 1179652
  108.1 93.4 %all-gather.8.cloned.1.call-start = ((), (), s32[]{:S(2)}) async-start(), calls=%async_computation.5 | async-start | bytes 1966080 | tf_op jit(solution)/shard_map/all_gather | solution.py:131
  172.6 100.3 %all-gather.10.cloned.1.call-start = ((), (), s32[]{:S(2)}) async-start(), calls=%async_computation.6 | async-start | bytes 8650752 | tf_op jit(solution)/shard_map/all_gather | solution.py:136
  173.1 169.4 %all-gather.12.cloned.1.call-start = ((), (), s32[]{:S(2)}) async-start(), calls=%async_computation.7 | async-start | bytes 8650752 | tf_op jit(solution)/shard_map/all_gather | solution.py:137
  173.7 238.5 %all-gather.14.cloned.1.call-start = ((), (), s32[]{:S(2)}) async-start(), calls=%async_computation.8 | async-start | bytes 8650752 | tf_op jit(solution)/shard_map/all_gather | solution.py:141
  174.3 293.2 %reduce-scatter.5.cloned.1.call-start = ((), (), s32[]{:S(2)}) async-start(), calls=%async_computation.9 | async-start | bytes 3932160 | tf_op jit(solution)/shard_map/reduce_scatter | solution.py:145
  412.2 57.2 %copy-start.1 = (bf16[512,2048]{1,0:T(8,128)(2,1)S(1)}, bf16[512,2048]{1,0:T(8,128)(2,1)}, u32[]{:S(2)}) copy-start(bf16[512,2048]{1,0:T(8,128)(2,1)} %param.20) | copy-start | bytes 6291460
Sparse Core Ops, SparseCore 0:
  16.3 27.0 all-gather.5
  108.2 61.6 reduce-scatter.2
  172.7 28.7 all-gather.7
  203.2 69.6 all-gather.9
  274.6 67.9 all-gather.11
  344.2 67.9 all-gather.13
  428.2 39.2 reduce-scatter.4
where the time goes:
time: 477 us; the launch traced here: 476 us
  waiting for transfers between devices  364 us (76%)
  matrix products  41 us (9%)
  local copies, waits for them, and re-layouts  27.2 us (6%)
  other arithmetic  16.8 us (4%)
  between operations  14.3 us (3%)
  starting transfers between devices  13 us (3%)
    all_gather x1, waiting for transfers between devices, local(): gate = add_rows(lax.all_gather(gate_weight, 'dp', axis=0, tiled=True))  71.4 us
    all_gather x1, waiting for transfers between devices, local(): lax.all_gather(down_weight, 'dp', axis=0, tiled=True)  69.7 us
    reduce_scatter x1, waiting for transfers between devices, local(): lax.psum_scatter(jnp.dot(mixed, output_weight, preferred_element_type=jnp...  61.6 us
    all_gather x1, waiting for transfers between devices, local(): upward = add_rows(lax.all_gather(up_weight, 'dp', axis=0, tiled=True))  60.6 us
    reduce_scatter x1, waiting for transfers between devices, local(): hidden_own = lax.psum_scatter(terms, 'mp', scatter_dimension=0, tiled=True)  39.4 us
    all_gather x1, waiting for transfers between devices, local(): normed_two = lax.all_gather(normed_own, 'mp', axis=0, tiled=True)  27.1 us
    ppermute x1, waiting for transfers between devices, swapped(): return lax.ppermute(value, axis, pairs)  25.3 us
    dot_general x1, matrix products, local(): lax.dot_general(activated, lax.all_gather(down_weight, 'dp', axis=0, tile...  15.9 us
  transfers between devices with their start and end apart: 9, of which 8 were waited for; matrix products, arithmetic and copies ran while one was open for 7% of the time, Pallas kernels for 0%

commit v1 on v0

--- a/solution.py
+++ b/solution.py
@@ -11,6 +11,16 @@
 CACHE = 512
 EPSILON = 1e-05
 ROPE_BASE = 10000.0
+
+
+def pass_along(x, axis, along):
+    peers = lax.axis_size(axis)
+    held, shards = (x, [x])
+    for _ in range(peers - 1):
+        held = lax.ppermute(held, axis, [(i, (i + 1) % peers) for i in range(peers)])
+        shards.insert(0, held)
+    line = jnp.concatenate(shards, axis=along)
+    return jnp.roll(line, (lax.axis_index(axis) + 1) * x.shape[along], axis=along)
 
 
 def swapped(value, axis, apart):
@@ -128,7 +138,7 @@
     )
     state_own = (tokens.astype(jnp.float32) + own_sum).astype(jnp.bfloat16)
     normed_own = layer_norm(state_own.astype(jnp.float32)).astype(jnp.bfloat16)
-    normed_two = lax.all_gather(normed_own, "mp", axis=0, tiled=True)
+    normed_two = pass_along(normed_own, "mp", 0)
 
     def add_rows(piece):
         return jnp.dot(normed_two, piece, preferred_element_type=jnp.float32)

time: 477 us -> 409 us (0.86)
  waiting for transfers between devices: 364 us -> 289 us
    all_gather x1, waiting for transfers between devices: 60.6 us -> 0.01 us  [local(): upward = add_rows(lax.all_gather(up_weight, 'dp', axis=0, tiled=True))]
    ppermute x0 -> x3, waiting for transfers between devices: none -> 30.9 us  [pass_along(): lax.ppermute(held, axis, [(i, (i + 1) % peers) for i in range(peers)])]
    all_gather x1 -> x0, waiting for transfers between devices: 27.1 us -> none  [local(): normed_two = lax.all_gather(normed_own, 'mp', axis=0, tiled=True)]
    all_gather x1, waiting for transfers between devices: 69.7 us -> 53.3 us  [local(): lax.all_gather(down_weight, 'dp', axis=0, tiled=True)]
  transfers between devices with their start and end apart: 9 -> 11, of which waited for: 8 -> 9; matrix products, arithmetic and copies ran while one was open for 7% -> 10% of each run, Pallas kernels for 0% -> 0%
where the time goes in v1:
time: 409 us
  waiting for transfers between devices  289 us (71%)
  matrix products  41.1 us (10%)
  local copies, waits for them, and re-layouts  31.9 us (8%)
  other arithmetic  18 us (4%)
  between operations  15.6 us (4%)
  starting transfers between devices  13 us (3%)
    all_gather x1, waiting for transfers between devices, local(): gate = add_rows(lax.all_gather(gate_weight, 'dp', axis=0, tiled=True))  70.7 us
    reduce_scatter x1, waiting for transfers between devices, local(): lax.psum_scatter(jnp.dot(mixed, output_weight, preferred_element_type=jnp...  59.8 us
    all_gather x1, waiting for transfers between devices, local(): lax.all_gather(down_weight, 'dp', axis=0, tiled=True)  53.3 us
    reduce_scatter x1, waiting for transfers between devices, local(): hidden_own = lax.psum_scatter(terms, 'mp', scatter_dimension=0, tiled=True)  40 us
    ppermute x3, waiting for transfers between devices, pass_along(): lax.ppermute(held, axis, [(i, (i + 1) % peers) for i in range(peers)])  30.9 us
    ppermute x1, waiting for transfers between devices, swapped(): return lax.ppermute(value, axis, pairs)  25.3 us
    dot_general x1, matrix products, local(): lax.dot_general(activated, lax.all_gather(down_weight, 'dp', axis=0, tile...  15.9 us
    reshape x1, local copies, waits for them, and re-layouts, local(): stored.reshape(stored.shape[0], 2, D)  9.46 us
  transfers between devices with their start and end apart: 11, of which 9 were waited for; matrix products, arithmetic and copies ran while one was open for 10% of the time, Pallas kernels for 0%

profile of v1, /device:TPU:1, one launch (start us, length us, event | category | flops | bytes accessed | tf_op | source)
XLA Modules:
  0.0 408.6 jit_solution(457913378124597812)
XLA Ops:
  9.1 7.8 %collective-permute-start = (bf16[128,4096]{0,1:T(8,128)(2,1)S(1)}, bf16[128,4096]{0,1:T(8,128)(2,1)}, u32[]{:S(2)}, u32[]{:S(2)}) collective-permute-start(bf16[128,4096]{0,1:T(8,128)(2,1)S(1)} %copy.71), channel_id=1, source_target_pairs={{0,128},{128,0},{1,129},{129,1},{2,130},{130,2},{3,131},{131,3},{4... | collective-permute-start | bytes 3145736 | tf_op jit(solution)/shard_map/ppermute | solution.py:29
  20.1 25.3 %collective-permute-done = bf16[128,4096]{0,1:T(8,128)(2,1)} collective-permute-done((bf16[128,4096]{0,1:T(8,128)(2,1)S(1)}, bf16[128,4096]{0,1:T(8,128)(2,1)}, u32[]{:S(2)}, u32[]{:S(2)}) %collective-permute-start) | collective-permute-done | bytes 1048608 | tf_op jit(solution)/shard_map/ppermute | solution.py:29
  46.7 9.5 %copy.73 = bf16[128,2,2048]{0,1,2:T(2,128)(2,1)} copy(bf16[128,2,2048]{0,2,1:T(8,128)(2,1)S(1)} %bitcast.26) | data formatting | bytes 2097152 | tf_op jit(solution)/shard_map/reshape | solution.py:111
  56.2 4.7 %all-to-all-start = ((bf16[128,2,2048]{0,1,2:T(2,128)(2,1)}), bf16[128,2,2048]{0,1,2:T(2,128)(2,1)S(1)}, u32[]{:S(2)}, u32[]{:S(2)}) async-start(bf16[128,2,2048]{0,1,2:T(2,128)(2,1)} %copy.73), calls=%async_computation | async-start | bytes 2097152 | tf_op jit(solution)/shard_map/all_to_all | solution.py:110
  63.3 7.3 %all-to-all-done = bf16[128,2,2048]{0,1,2:T(2,128)(2,1)S(1)} async-done(((bf16[128,2,2048]{0,1,2:T(2,128)(2,1)}), bf16[128,2,2048]{0,1,2:T(2,128)(2,1)S(1)}, u32[]{:S(2)}, u32[]{:S(2)}) %all-to-all-start) | async-done | bytes 1048608 | tf_op jit(solution)/shard_map/all_to_all | solution.py:110
  75.8 2.0 copy.76
  79.7 2.0 fusion.4
  81.7 3.5 fusion.47
  86.6 4.0 fusion.49
  90.6 2.3 reshape.151
  92.9 3.9 convolution_convert_fusion
  98.7 2.3 fusion.53
  102.4 2.7 fusion.55
  106.2 2.8 fusion.56
  111.0 59.8 %reduce-scatter.3.cloned.1.call-done = f32[96,2048]{1,0:T(8,128)} async-done(((f32[384,2048]{1,0:T(8,128)}), f32[96,2048]{1,0:T(8,128)}) %reduce-scatter.3.cloned.1.call-update) | async-done | bytes 786448 | tf_op jit(solution)/shard_map/reduce_scatter | solution.py:133
  172.8 11.2 %collective-permute-done.1 = bf16[96,2048]{1,0:T(8,128)(2,1)S(1)} collective-permute-done((bf16[96,2048]{1,0:T(8,128)(2,1)S(1)}, bf16[96,2048]{1,0:T(8,128)(2,1)S(1)}, u32[]{:S(2)}, u32[]{:S(2)}) %collective-permute-start.1) | collective-permute-done | bytes 393248 | tf_op jit(solution)/shard_map/ppermute | solution.py:20
  184.0 10.3 %collective-permute-done.2 = bf16[96,2048]{1,0:T(8,128)(2,1)S(1)} collective-permute-done((bf16[96,2048]{1,0:T(8,128)(2,1)S(1)}, bf16[96,2048]{1,0:T(8,128)(2,1)S(1)}, u32[]{:S(2)}, u32[]{:S(2)}) %collective-permute-start.2) | collective-permute-done | bytes 393248 | tf_op jit(solution)/shard_map/ppermute | solution.py:20
  194.3 9.4 %collective-permute-done.3 = bf16[96,2048]{1,0:T(8,128)(2,1)S(1)} collective-permute-done((bf16[96,2048]{1,0:T(8,128)(2,1)S(1)}, bf16[96,2048]{1,0:T(8,128)(2,1)S(1)}, u32[]{:S(2)}, u32[]{:S(2)}) %collective-permute-start.3) | collective-permute-done | bytes 393248 | tf_op jit(solution)/shard_map/ppermute | solution.py:20
  210.4 9.0 %fusion.12 = f32[384,2048]{1,0:T(8,128)} fusion(bf16[2048,2048]{1,0:T(8,128)(2,1)} %all-gather.9.cloned.1.call-done, bf16[768,2048]{1,0:T(8,128)(2,1)} %constant_dynamic-update-slice_fusion, s32[]{:T(128)S(6)} %select_n.37), kind=kOutput, calls=%fused_computation.18 | convolution fusion | flops 3221225472 | bytes 13107204 | tf_op jit(solution)/shard_map/dot_general | solution.py:144
  219.5 53.3 %all-gather.11.cloned.1.call-done = bf16[2048,2048]{1,0:T(8,128)(2,1)} async-done(((bf16[64,2048]{1,0:T(8,128)(2,1)}), bf16[2048,2048]{1,0:T(8,128)(2,1)}) %all-gather.11.cloned.1.call-update) | async-done | bytes 8388624 | tf_op jit(solution)/shard_map/all_gather | solution.py:151
  272.8 70.7 %all-gather.7.cloned.1.call-done = bf16[2048,2048]{1,0:T(8,128)(2,1)} async-done(((bf16[64,2048]{1,0:T(8,128)(2,1)}), bf16[2048,2048]{1,0:T(8,128)(2,1)}) %all-gather.7.cloned.1.call-update) | async-done | bytes 8388624 | tf_op jit(solution)/shard_map/all_gather | solution.py:146
  343.4 15.9 %fusion.10 = f32[384,2048]{1,0:T(8,128)} fusion(bf16[2048,2048]{1,0:T(8,128)(2,1)} %all-gather.11.cloned.1.call-done, f32[384,2048]{1,0:T(8,128)} %fusion.12, bf16[2048,2048]{1,0:T(8,128)(2,1)} %all-gather.7.cloned.1.call-done, bf16[768,2048]{1,0:T(8,128)(2,1)} %constant_dynamic-update-slice_fusion, s32[]{:T(128)S(6)} %select_n.37), kind=kOutput, calls=%fused_computation.16 | convolution fusion | flops 6447169536 | bytes 24641540 | tf_op jit(solution)/shard_map/dot_general | solution.py:149
  359.3 40.0 %reduce-scatter.5.cloned.1.call-done = f32[96,2048]{1,0:T(8,128)} async-done(((f32[384,2048]{1,0:T(8,128)}), f32[96,2048]{1,0:T(8,128)}) %reduce-scatter.5.cloned.1.call-update) | async-done | bytes 786448 | tf_op jit(solution)/shard_map/reduce_scatter | solution.py:155
  399.3 2.0 fusion.34
  (78 shorter events, 31.3 us)
Async XLA Ops:
  7.4 98.9 %copy-start = (bf16[512,2048]{1,0:T(8,128)(2,1)S(1)}, bf16[512,2048]{1,0:T(8,128)(2,1)}, u32[]{:S(2)}) copy-start(bf16[512,2048]{1,0:T(8,128)(2,1)} %param.20) | copy-start | bytes 6291460
  7.4 70.5 %all-gather.5.cloned.1.call-start = ((), (), s32[]{:S(2)}) async-start(), calls=%async_computation.3 | async-start | bytes 1966080 | tf_op jit(solution)/shard_map/all_gather | solution.py:115
  9.1 36.3 %collective-permute-start = (bf16[128,4096]{0,1:T(8,128)(2,1)S(1)}, bf16[128,4096]{0,1:T(8,128)(2,1)}, u32[]{:S(2)}, u32[]{:S(2)}) collective-permute-start(bf16[128,4096]{0,1:T(8,128)(2,1)S(1)} %copy.71), channel_id=1, source_target_pairs={{0,128},{128,0},{1,129},{129,1},{2,130},{130,2},{3,131},{131,3},{4... | collective-permute-start | bytes 3145736 | tf_op jit(solution)/shard_map/ppermute | solution.py:29
  56.2 14.5 %all-to-all-start = ((bf16[128,2,2048]{0,1,2:T(2,128)(2,1)}), bf16[128,2,2048]{0,1,2:T(2,128)(2,1)S(1)}, u32[]{:S(2)}, u32[]{:S(2)}) async-start(bf16[128,2,2048]{0,1,2:T(2,128)(2,1)} %copy.73), calls=%async_computation | async-start | bytes 2097152 | tf_op jit(solution)/shard_map/all_to_all | solution.py:110
  60.9 109.9 %reduce-scatter.3.cloned.1.call-start = ((), (), s32[]{:S(2)}) async-start(), calls=%async_computation.4 | async-start | bytes 3932160 | tf_op jit(solution)/shard_map/reduce_scatter | solution.py:133
  77.9 3.8 copy-start.2
  98.7 2.3 copy-start.4
  98.7 2.3 copy-start.5
  101.4 1.0 copy-start.8
  102.4 2.7 copy-start.6
  102.4 2.7 copy-start.7
  109.0 61.8 %copy-start.3 = (bf16[96,2048]{1,0:T(8,128)(2,1)S(1)}, bf16[96,2048]{1,0:T(8,128)(2,1)}, u32[]{:S(2)}) copy-start(bf16[96,2048]{1,0:T(8,128)(2,1)} %param.12) | copy-start | bytes 1179652
  109.0 101.4 %all-gather.9.cloned.1.call-start = ((), (), s32[]{:S(2)}) async-start(), calls=%async_computation.6 | async-start | bytes 8650752 | tf_op jit(solution)/shard_map/all_gather | solution.py:147
  109.6 163.2 %all-gather.11.cloned.1.call-start = ((), (), s32[]{:S(2)}) async-start(), calls=%async_computation.7 | async-start | bytes 8650752 | tf_op jit(solution)/shard_map/all_gather | solution.py:151
  110.2 233.2 %all-gather.7.cloned.1.call-start = ((), (), s32[]{:S(2)}) async-start(), calls=%async_computation.5 | async-start | bytes 8650752 | tf_op jit(solution)/shard_map/all_gather | solution.py:146
  110.8 288.6 %reduce-scatter.5.cloned.1.call-start = ((), (), s32[]{:S(2)}) async-start(), calls=%async_computation.8 | async-start | bytes 3932160 | tf_op jit(solution)/shard_map/reduce_scatter | solution.py:155
  172.7 11.3 %collective-permute-start.1 = (bf16[96,2048]{1,0:T(8,128)(2,1)S(1)}, bf16[96,2048]{1,0:T(8,128)(2,1)S(1)}, u32[]{:S(2)}, u32[]{:S(2)}) collective-permute-start(bf16[96,2048]{1,0:T(8,128)(2,1)S(1)} %fusion.33), channel_id=1, source_target_pairs={{0,1},{1,2},{2,3},{3,0},{4,5},{5,6},{6,7},{7,4},{8,9},{9,10},{10,1... | collective-permute-start | bytes 1179656 | tf_op jit(solution)/shard_map/ppermute | solution.py:20
  184.0 10.3 %collective-permute-start.2 = (bf16[96,2048]{1,0:T(8,128)(2,1)S(1)}, bf16[96,2048]{1,0:T(8,128)(2,1)S(1)}, u32[]{:S(2)}, u32[]{:S(2)}) collective-permute-start(bf16[96,2048]{1,0:T(8,128)(2,1)S(1)} %collective-permute-done.1), channel_id=1, source_target_pairs={{0,1},{1,2},{2,3},{3,0},{4,5},{5,6},{6,7},{7,4},{8,9},{9,10},{10,1... | collective-permute-start | bytes 1179656 | tf_op jit(solution)/shard_map/ppermute | solution.py:20
  194.3 9.4 %collective-permute-start.3 = (bf16[96,2048]{1,0:T(8,128)(2,1)S(1)}, bf16[96,2048]{1,0:T(8,128)(2,1)S(1)}, u32[]{:S(2)}, u32[]{:S(2)}) collective-permute-start(bf16[96,2048]{1,0:T(8,128)(2,1)S(1)} %collective-permute-done.2), channel_id=1, source_target_pairs={{0,1},{1,2},{2,3},{3,0},{4,5},{5,6},{6,7},{7,4},{8,9},{9,10},{10,1... | collective-permute-start | bytes 1179656 | tf_op jit(solution)/shard_map/ppermute | solution.py:20
  343.4 57.9 %copy-start.1 = (bf16[512,2048]{1,0:T(8,128)(2,1)S(1)}, bf16[512,2048]{1,0:T(8,128)(2,1)}, u32[]{:S(2)}) copy-start(bf16[512,2048]{1,0:T(8,128)(2,1)} %param.20) | copy-start | bytes 6291460
Sparse Core Ops, SparseCore 0:
  17.1 27.0 all-gather.4
  109.1 61.6 reduce-scatter.2
  359.5 39.8 reduce-scatter.4
Sparse Core Ops, SparseCore 1:
  111.4 91.0 all-gather.8
  204.1 68.6 all-gather.10
  274.5 68.9 all-gather.6
